TPU v7x, 512 devices: a whole 4x8x8 slice. The times are simulated.
512 devices in a mesh: gx: 64 (over x, z, y_hi), gy: 8 (over y_lo, core).
Axes of the slice: x: 4, y: 8 (y_hi: 2, y_lo: 4; y = y_hi * 4 + y_lo), z: 8, core: 2. Of those that a mesh axis runs over, the one named last changes fastest.
Arguments:
- velocity: float32 [3, 128, 1024, 128], P(None, 'gx', 'gy'), may hold values from -4 to 4.5, as said below
- previous: float32 [3, 128, 1024, 128], P(None, 'gx', 'gy'), may hold values from -1800 to 1800
Outputs:
- advanced: float32 [3, 128, 1024, 128], P(None, 'gx', 'gy')
Inputs may be any that keep to these rules, and one draw needn't show every extreme that they name: `velocity`: each component is zero on the two walls, the first and the last wall-normal point.
All inputs are finite; a program needn't handle non-finite values.
Results may differ from a plain program's by a relative error of at most 0.0003.
Values sent between devices are 32-bit elements; how exact they have to be, the bound alone decides.
A program may use at most 64 MiB of HBM per device.

v0:
```python
import jax
import jax.numpy as jnp
from jax import lax
from jax.sharding import PartitionSpec as P

NY = 1024


LENGTH_SPACING = 8.0 * 3.141592653589793 / 4096.0
SPAN_SPACING = 3.0 * 3.141592653589793 / 3072.0
VISCOSITY = 1.0 / 2000.0
TIME_STEP = 0.003
GAMMA_NOW = 5.0 / 12.0
ZETA_PAST = -17.0 / 60.0


def padded(cells, sides, width):
    for axis, dim in sides:
        count = lax.axis_size(axis)
        head = lax.slice_in_dim(cells, 0, width, axis=dim)
        tail = lax.slice_in_dim(cells, cells.shape[dim] - width, cells.shape[dim], axis=dim)
        cells = jnp.concatenate(
            [
                lax.ppermute(tail, axis, [(i, (i + 1) % count) for i in range(count)]),
                cells,
                lax.ppermute(head, axis, [((i + 1) % count, i) for i in range(count)]),
            ],
            axis=dim,
        )
    return cells


def chebyshev_rows(total, count):
    row_ids = jnp.arange(count, dtype=jnp.int32)
    col_ids = jnp.arange(total, dtype=jnp.int32)
    row_angle = jnp.pi * row_ids.astype(jnp.float32) / (total - 1)
    col_angle = jnp.pi * col_ids.astype(jnp.float32) / (total - 1)
    on_diagonal = row_ids[:, None] == col_ids[None, :]
    parity = (row_ids[:, None] + col_ids[None, :]) % 2
    signs = 1.0 - 2.0 * parity.astype(jnp.float32)
    row_half = jnp.where((row_ids == 0) | (row_ids == total - 1), 0.5, 1.0).astype(jnp.float32)
    col_half = jnp.where((col_ids == 0) | (col_ids == total - 1), 0.5, 1.0).astype(jnp.float32)
    weight_ratio = signs * col_half[None, :] / row_half[:, None]
    spacing = (
        -2.0
        * jnp.sin(0.5 * (row_angle[:, None] + col_angle[None, :]))
        * jnp.sin(0.5 * (row_angle[:, None] - col_angle[None, :]))
    )
    spacing_safe = jnp.where(on_diagonal, 1.0, spacing)
    first_off = jnp.where(on_diagonal, 0.0, weight_ratio / spacing_safe)
    first_diag = -jnp.sum(first_off, axis=1)
    first = first_off + jnp.where(on_diagonal, first_diag[:, None], 0.0)
    second_off = jnp.where(
        on_diagonal, 0.0, 2.0 * first_off * (first_diag[:, None] - 1.0 / spacing_safe)
    )
    second = second_off + jnp.where(on_diagonal, -jnp.sum(second_off, axis=1)[:, None], 0.0)
    return (first, second)


def central(center, plus_one, minus_one, plus_two, minus_two, spacing):
    first = (8.0 * (plus_one - minus_one) - (plus_two - minus_two)) / (12.0 * spacing)
    second = (16.0 * (plus_one + minus_one) - (plus_two + minus_two) - 30.0 * center) / (
        12.0 * spacing * spacing
    )
    return (first, second)


def shards(velocity, previous):
    widened = padded(velocity, (("gx", 1),), 2)
    along_x, across_x = central(
        widened[:, 2:-2],
        widened[:, 3:-1],
        widened[:, 1:-3],
        widened[:, 4:],
        widened[:, :-4],
        LENGTH_SPACING,
    )
    along_z, across_z = central(
        velocity,
        jnp.roll(velocity, -1, 3),
        jnp.roll(velocity, 1, 3),
        jnp.roll(velocity, -2, 3),
        jnp.roll(velocity, 2, 3),
        SPAN_SPACING,
    )
    plane_term = (
        VISCOSITY * (across_x + across_z) - velocity[0:1] * along_x - velocity[2:3] * along_z
    )
    first_matrix, second_matrix = chebyshev_rows(NY, NY)
    operators = jnp.concatenate([first_matrix, second_matrix], axis=0)
    stacked = jnp.einsum(
        "ky,cxyz->cxkz",
        operators,
        lax.all_to_all(velocity, "gy", split_axis=3, concat_axis=2, tiled=True),
        precision=lax.Precision.HIGHEST,
    )
    wall_first = stacked[:, :, :NY]
    wall_second = stacked[:, :, NY:]
    joined = jnp.concatenate([wall_first, wall_second], axis=0)
    returned = lax.all_to_all(joined, "gy", split_axis=2, concat_axis=3, tiled=True)
    wall_term = VISCOSITY * returned[3:] - velocity[1:2] * returned[:3]
    tendency = plane_term + wall_term
    return velocity + TIME_STEP * (GAMMA_NOW * tendency + ZETA_PAST * previous)


def solution(mesh):
    in_specs = (P(None, "gx", "gy", None), P(None, "gx", "gy", None))
    out_specs = P(None, "gx", "gy", None)
    return jax.shard_map(shards, mesh=mesh, in_specs=in_specs, out_specs=out_specs, check_vma=False)
```

profile of v0, /device:TPU:1, one launch (start us, length us, event | category | flops | bytes accessed | tf_op | source)
XLA Modules:
  0.0 222.1 jit_solution(3157512944868528438)
XLA Ops:
  0.0 1.9 copy.66
  1.9 10.2 %all-to-all-start = ((f32[3,2,128,128]{2,1,0,3:T(2,128)}), f32[3,2,128,128]{2,1,0,3:T(2,128)S(1)}, u32[]{:S(2)}, u32[]{:S(2)}) async-start(f32[3,2,128,128]{2,1,0,3:T(2,128)} %copy.66), calls=%async_computation | async-start | bytes 786432 | tf_op jit(solution)/shard_map/all_to_all | solution.py:94
  12.1 32.4 %fusion.18 = f32[1024]{0:T(1024)S(1)} fusion(f32[1024]{0:T(1024)S(1)} %get-tuple-element.22, f32[1024]{0:T(1024)S(1)} %get-tuple-element.23), kind=kLoop, calls=%fused_computation.24 | loop fusion | flops 29359104 | bytes 12288 | tf_op jit(solution)/shard_map/reduce_sum | solution.py:51
  44.5 32.8 %fusion.19 = f32[1024]{0:T(1024)S(1)} fusion(f32[1024]{0:T(1024)S(1)} %neg.15, f32[1024]{0:T(1024)S(1)} %get-tuple-element.22, f32[1024]{0:T(1024)S(1)} %get-tuple-element.23), kind=kLoop, calls=%fused_computation.25 | loop fusion | flops 34601984 | bytes 16384 | tf_op jit(solution)/shard_map/reduce_sum | solution.py:56
  77.3 35.1 %fusion.9 = (f32[1024,1024]{1,0:T(8,128)}, f32[1024,1024]{1,0:T(8,128)}) fusion(f32[1024]{0:T(1024)S(1)} %neg.15, f32[1024]{0:T(1024)S(1)} %get-tuple-element.22, f32[1024]{0:T(1024)S(1)} %get-tuple-element.23, f32[1024]{0:T(1024)S(1)} %neg.16), kind=kLoop, calls=%fused_computation.15 | loop fusion | flops 37748736 | bytes 8404992 | tf_op jit(solution)/shard_map/add | solution.py:52
  112.5 10.8 %fusion.17 = f32[3,2,2048,16]{2,3,1,0:T(8,128)S(1)} fusion(f32[1024,1024]{1,0:T(8,128)} %get-tuple-element.21, f32[1024,1024]{1,0:T(8,128)} %get-tuple-element.20, f32[3,2,8,2,8,128]{5,4,3,2,1,0:T(8,128)S(1)} %bitcast.45), kind=kOutput, calls=%fused_computation.23 | convolution fusion | flops 2418016256 | bytes 9568256 | tf_op jit(solution)/shard_map/ky,cxyz->cxkz/dot_general | solution.py:91
  123.4 6.6 %copy.69 = f32[6,2,1024,16]{3,1,0,2:T(2,128)} copy(f32[6,2,1024,16]{2,3,1,0:T(8,128)S(1)} %pad_maximum_fusion) | data formatting | bytes 1572864 | tf_op jit(solution)/shard_map/concatenate | solution.py:99
  130.0 10.8 %reshape.42 = f32[8,1,24576]{2,1,0:T(1,128)} reshape(f32[1024,6,2,16]{3,2,1,0:T(2,128)} %bitcast.42) | data formatting | bytes 1572864
  140.8 5.1 %all-to-all-start.1 = ((f32[8,1,24576]{2,1,0:T(1,128)}), f32[8,1,24576]{2,1,0:T(1,128)S(1)}, u32[]{:S(2)}, u32[]{:S(2)}) async-start(f32[8,1,24576]{2,1,0:T(1,128)} %reshape.42), calls=%async_computation.1 | async-start | bytes 1572864 | tf_op jit(solution)/shard_map/all_to_all | solution.py:100
  145.9 0.2 copy.75
  146.1 12.8 %collective-permute-start = (f32[3,2,128,128]{2,3,1,0:T(8,128)S(1)}, f32[3,2,128,128]{2,3,1,0:T(8,128)}, u32[]{:S(2)}, u32[]{:S(2)}) collective-permute-start(f32[3,2,128,128]{2,3,1,0:T(8,128)S(1)} %copy.75), channel_id=1, source_target_pairs={{8,0},{16,8},{24,16},{32,24},{40,32},{48,40},{56,48},{64,56},{72,6... | collective-permute-start | bytes 1179656 | tf_op jit(solution)/shard_map/ppermute | solution.py:26
  158.9 1.9 collective-permute-start.1
  160.8 0.8 copy.64
  161.6 0.7 copy.65
  162.3 0.7 copy.72
  163.3 0.8 fusion.34
  164.1 0.6 fusion.33
  164.7 35.0 %all-to-all-done.1 = f32[8,1,24576]{2,1,0:T(1,128)S(1)} async-done(((f32[8,1,24576]{2,1,0:T(1,128)}), f32[8,1,24576]{2,1,0:T(1,128)S(1)}, u32[]{:S(2)}, u32[]{:S(2)}) %all-to-all-start.1) | async-done | bytes 786464 | tf_op jit(solution)/shard_map/all_to_all | solution.py:100
  199.7 0.6 broadcast.158
  200.2 2.5 %reduce = f32[8,24576]{1,0:T(8,128)S(1)} reduce(f32[8,1,24576]{2,1,0:T(1,128)S(1)} %all-to-all-done.1, f32[]{:T(128)} %broadcast.158), dimensions={1}, to_apply=%all_to_all.28.reduce_sub_computation | reduce | bytes 1572868 | tf_op jit(solution)/shard_map/all_to_all | solution.py:100
  202.7 11.1 %reshape.43 = f32[1024,6,2,16]{3,2,1,0:T(2,128)} reshape(f32[8,24576]{1,0:T(8,128)S(1)} %reduce) | data formatting | bytes 1572864
  213.8 5.1 %copy.78 = f32[6,2,8,128,16]{3,2,4,1,0:T(8,128)S(1)} copy(f32[6,2,8,128,16]{4,1,0,3,2:T(2,128)} %bitcast.43) | data formatting | bytes 1572864 | tf_op jit(solution)/shard_map/all_to_all | solution.py:100
  219.2 2.0 fusion.27
  221.2 0.9 copy.76
  (22 shorter events, 0.6 us)
Async XLA Ops:
  1.9 110.5 %all-to-all-start = ((f32[3,2,128,128]{2,1,0,3:T(2,128)}), f32[3,2,128,128]{2,1,0,3:T(2,128)S(1)}, u32[]{:S(2)}, u32[]{:S(2)}) async-start(f32[3,2,128,128]{2,1,0,3:T(2,128)} %copy.66), calls=%async_computation | async-start | bytes 786432 | tf_op jit(solution)/shard_map/all_to_all | solution.py:94
  130.0 15.9 %copy-start = (f32[3,2,128,128]{3,2,1,0:T(8,128)S(1)}, f32[3,2,128,128]{3,2,1,0:T(8,128)}, u32[]{:S(2)}) copy-start(f32[3,2,128,128]{3,2,1,0:T(8,128)} %param.2) | copy-start | bytes 1179652
  130.0 33.1 %copy-start.2 = (f32[3,2,128,128]{3,2,1,0:T(8,128)S(1)}, f32[3,2,128,128]{3,2,1,0:T(8,128)}, u32[]{:S(2)}) copy-start(f32[3,2,128,128]{3,2,1,0:T(8,128)} %param.3) | copy-start | bytes 1179652
  140.8 58.9 %all-to-all-start.1 = ((f32[8,1,24576]{2,1,0:T(1,128)}), f32[8,1,24576]{2,1,0:T(1,128)S(1)}, u32[]{:S(2)}, u32[]{:S(2)}) async-start(f32[8,1,24576]{2,1,0:T(1,128)} %reshape.42), calls=%async_computation.1 | async-start | bytes 1572864 | tf_op jit(solution)/shard_map/all_to_all | solution.py:100
  146.1 73.1 %collective-permute-start = (f32[3,2,128,128]{2,3,1,0:T(8,128)S(1)}, f32[3,2,128,128]{2,3,1,0:T(8,128)}, u32[]{:S(2)}, u32[]{:S(2)}) collective-permute-start(f32[3,2,128,128]{2,3,1,0:T(8,128)S(1)} %copy.75), channel_id=1, source_target_pairs={{8,0},{16,8},{24,16},{32,24},{40,32},{48,40},{56,48},{64,56},{72,6... | collective-permute-start | bytes 1179656 | tf_op jit(solution)/shard_map/ppermute | solution.py:26
  158.9 60.3 %collective-permute-start.1 = (f32[3,2,128,128]{2,3,1,0:T(8,128)S(1)}, f32[3,2,128,128]{2,3,1,0:T(8,128)}, u32[]{:S(2)}, u32[]{:S(2)}) collective-permute-start(f32[3,2,128,128]{2,3,1,0:T(8,128)S(1)} %copy.75), channel_id=1, source_target_pairs={{0,8},{8,16},{16,24},{24,32},{32,40},{40,48},{48,56},{56,64},{64,7... | collective-permute-start | bytes 1179656 | tf_op jit(solution)/shard_map/ppermute | solution.py:24
  213.8 5.4 %copy-start.1 = (f32[3,2,128,126]{2,3,1,0:T(8,128)S(1)}, f32[3,2,128,126]{2,3,1,0:T(8,128)}, u32[]{:S(2)}) copy-start(f32[3,2,128,126]{2,3,1,0:T(8,128)} %get-tuple-element.17) | copy-start | bytes 1161220
where the time goes:
time: 223 us; the launch traced here: 222 us
  other arithmetic  105 us (47%)
  local copies, waits for them, and re-layouts  41.2 us (18%)
  waiting for transfers between devices  35 us (16%)
  starting transfers between devices  30 us (13%)
  matrix products  10.8 us (5%)
    add x1, other arithmetic, chebyshev_rows(): first = first_off + jnp.where(on_diagonal, first_diag[:, None], 0.0)  35.1 us
    all_to_all x1, waiting for transfers between devices, shards(): lax.all_to_all(joined, 'gy', split_axis=2, concat_axis=3, tiled=True)  35 us
    reduce_sum x1, other arithmetic, chebyshev_rows(): jnp.sum(second_off, axis=1)[:, None]  32.8 us
    reduce_sum x1, other arithmetic, chebyshev_rows(): first_diag = -jnp.sum(first_off, axis=1)  32.4 us
    unnamed x11, local copies, waits for them, and re-layouts  24.1 us
    ppermute x1, starting transfers between devices, padded(): lax.ppermute(head, axis, [((i + 1) % count, i) for i in range(count)])  12.8 us
    dot_general x1, matrix products, shards(): jnp.einsum('ky,cxyz->cxkz', operators, lax.all_to_all(velocity, 'gy', spl...  10.8 us
    all_to_all x1, starting transfers between devices, shards(): lax.all_to_all(velocity, 'gy', split_axis=3, concat_axis=2, tiled=True)  10.2 us
  transfers between devices with their start and end apart: 4, of which 1 were waited for; matrix products, arithmetic and copies ran while one was open for 56% of the time, Pallas kernels for 0%

commit v1 on v0

v1 whole, which is shorter than its diff:
```python
import functools

import jax
import jax.numpy as jnp
import numpy as np
from jax import lax
from jax.experimental import pallas as pl
from jax.experimental.pallas import tpu as pltpu
from jax.sharding import PartitionSpec as P

NY = 1024
PARTS = 8
HALVES = 2
RANKS = PARTS * HALVES
CHUNKS = 4

LENGTH_SPACING = 8.0 * 3.141592653589793 / 4096.0
SPAN_SPACING = 3.0 * 3.141592653589793 / 3072.0
VISCOSITY = 1.0 / 2000.0
TIME_STEP = 0.003
GAMMA_NOW = 5.0 / 12.0
ZETA_PAST = -17.0 / 60.0
NOW = TIME_STEP * GAMMA_NOW
MESH = pl.DeviceIdType.MESH


def chebyshev_rows(total):
    f32 = np.float32
    ids = np.arange(total)
    angle = (f32(np.pi) * ids.astype(f32)) / f32(total - 1)
    on_diagonal = np.eye(total, dtype=bool)
    signs = (1.0 - 2.0 * ((ids[:, None] + ids[None, :]) % 2)).astype(f32)
    half = np.where((ids == 0) | (ids == total - 1), 0.5, 1.0).astype(f32)
    weight_ratio = signs * half[None, :] / half[:, None]
    plus = f32(0.5) * (angle[:, None] + angle[None, :])
    minus = f32(0.5) * (angle[:, None] - angle[None, :])
    spacing = f32(-2.0) * np.sin(plus) * np.sin(minus)
    safe = np.where(on_diagonal, f32(1.0), spacing)
    off = np.where(on_diagonal, f32(0.0), weight_ratio / safe).astype(np.float64)
    diag = -off.sum(axis=1)
    first = off + np.where(on_diagonal, diag[:, None], 0.0)
    off2 = np.where(on_diagonal, 0.0, 2.0 * off * (diag[:, None] - 1.0 / safe))
    second = off2 + np.where(on_diagonal, -off2.sum(axis=1)[:, None], 0.0)
    return first, second


@functools.lru_cache(maxsize=1)
def operators():
    first, second = chebyshev_rows(NY)
    first = (first * NOW).T.reshape(CHUNKS, 256, PARTS, 128)
    second = (second * (NOW * VISCOSITY)).T.reshape(CHUNKS, 256, PARTS, 128)
    both = np.concatenate([first, second], axis=3).transpose(0, 2, 1, 3)
    high = both.astype(np.float32).astype(jnp.bfloat16)
    low = (both - high.astype(np.float64)).astype(np.float32).astype(jnp.bfloat16)
    return np.stack([high, low])


def kernel(lines, vel_hbm, prev_hbm, op_hbm, out, vel, prev, op, send, recv, below, above, acc, reply, back,
           local_sem, send_sem, recv_sem, halo_send, halo_recv, reply_sem, back_sem):
    gx, gy = lax.axis_index("gx"), lax.axis_index("gy")
    line, half = gx // 2, gx % 2
    me = half * PARTS + gy
    pair = gy // 2
    nxt, prv = lax.rem(line + 1, lines), lax.rem(line + lines - 1, lines)

    def device(rank):
        return (line * 2 + rank // PARTS, lax.rem(rank, PARTS))

    load_vel = pltpu.make_async_copy(vel_hbm, vel, local_sem.at[0])
    load_prev = pltpu.make_async_copy(prev_hbm, prev, local_sem.at[1])
    load_op = pltpu.make_async_copy(op_hbm, op, local_sem.at[2])
    load_vel.start()
    load_prev.start()
    load_op.start()

    barrier = pltpu.get_barrier_semaphore()
    for k in range(1, RANKS):
        pl.semaphore_signal(barrier, inc=1, device_id=device(lax.rem(me + k, RANKS)), device_id_type=MESH)
    for other in (nxt, prv):
        pl.semaphore_signal(barrier, inc=1, device_id=(other * 2 + half, gy), device_id_type=MESH)

    load_vel.wait()
    for c in range(3):
        for p in range(2):
            send[:, c, p] = vel[c, p].T.reshape(RANKS, 8, 128)
    pl.semaphore_wait(barrier, RANKS + 1)

    def out_copy(source, target):
        return pltpu.make_async_remote_copy(
            src_ref=send.at[target], dst_ref=recv.at[source], send_sem=send_sem.at[target],
            recv_sem=recv_sem.at[source], device_id=device(target), device_id_type=MESH)

    def others(shift):
        chip = lax.rem(pair + shift + CHUNKS, CHUNKS)
        found = []
        for h in range(HALVES):
            for core in range(2):
                if shift == 0 and h == 0 and core == 0:
                    continue
                hh = lax.rem(half + h, 2) if shift == 0 else h
                cc = lax.rem(gy + core, 2) if shift == 0 else core
                found.append(hh * PARTS + chip * 2 + cc)
        return found

    for j in (1, 3, 2, 0):
        for target in others(-j):
            out_copy(me, target).start()
    recv[me] = send[me]

    load_prev.wait()
    for p in range(2):
        w = vel[2, p]
        for c in range(3):
            f = vel[c, p]
            up, down = pltpu.roll(f, 127, 1), pltpu.roll(f, 1, 1)
            up2, down2 = pltpu.roll(f, 126, 1), pltpu.roll(f, 2, 1)
            dz = (8.0 * (up - down) - (up2 - down2)) * (NOW / (12.0 * SPAN_SPACING))
            dzz = (16.0 * (up + down) - (up2 + down2) - 30.0 * f) * (
                NOW * VISCOSITY / (12.0 * SPAN_SPACING * SPAN_SPACING))
            out[c, p] = f + dzz - w * dz + (TIME_STEP * ZETA_PAST) * prev[c, p]
    load_op.wait()

    def halo_copies(chip):
        rows = pl.ds(chip * 2, 2)
        up = pltpu.make_async_remote_copy(
            src_ref=recv.at[pl.ds(PARTS + chip * 2, 2)], dst_ref=below.at[rows], send_sem=halo_send.at[0, chip],
            recv_sem=halo_recv.at[0, chip], device_id=(nxt * 2 + half, gy), device_id_type=MESH)
        down = pltpu.make_async_remote_copy(
            src_ref=recv.at[rows], dst_ref=above.at[rows], send_sem=halo_send.at[1, chip],
            recv_sem=halo_recv.at[1, chip], device_id=(prv * 2 + half, gy), device_id_type=MESH)
        return up, down

    def products(chip):
        a = jnp.concatenate([
            jnp.concatenate([recv[h * PARTS + chip * 2 + core].reshape(48, 128) for core in range(2)], axis=1)
            for h in range(HALVES)], axis=0)
        high = a.astype(jnp.bfloat16)
        low = (a - high.astype(jnp.float32)).astype(jnp.bfloat16)
        stacked = jnp.concatenate([high, low], axis=0)

        def product(n):
            coarse = jnp.dot(stacked, op[0, chip, n], preferred_element_type=jnp.float32)
            fine = jnp.dot(high, op[1, chip, n], preferred_element_type=jnp.float32)
            return coarse[:96] + (coarse[96:] + fine)

        return product

    def reply_copy(source, target):
        return pltpu.make_async_remote_copy(
            src_ref=reply.at[target], dst_ref=back.at[source], send_sem=reply_sem.at[target],
            recv_sem=back_sem.at[source], device_id=device(target), device_id_type=MESH)

    order = (0, 1, 3, 2)
    for step, j in enumerate(order):
        chip = lax.rem(pair + j, CHUNKS)
        for source in others(j):
            out_copy(source, me).wait_recv()
        for copy in halo_copies(chip):
            copy.start()
        product = products(chip)
        if step < CHUNKS - 1:
            @pl.loop(0, PARTS)
            def _(n, product=product, step=step):
                if step == 0:
                    acc[n] = product(n)
                else:
                    acc[n] += product(n)

    def finish(n):
        walls = (acc[n] + product(n)).reshape(HALVES, 3, 2, 8, 256)
        fields = [[None] * 6 for _ in range(3)]
        for c in range(3):
            for p in range(2):
                fields[c][p] = below[n, c, p]
                fields[c][p + 2] = recv[n, c, p]
                fields[c][p + 4] = recv[PARTS + n, c, p]
            planes = fields[c] + [above[n, c, 0], above[n, c, 1]]
            fields[c] = planes
        for h in range(HALVES):
            for p in range(2):
                at = 2 + 2 * h + p
                u, v = fields[0][at], fields[1][at]
                for c in range(3):
                    f = fields[c]
                    dx = (8.0 * (f[at + 1] - f[at - 1]) - (f[at + 2] - f[at - 2])) * (
                        NOW / (12.0 * LENGTH_SPACING))
                    dxx = (16.0 * (f[at + 1] + f[at - 1]) - (f[at + 2] + f[at - 2]) - 30.0 * f[at]) * (
                        NOW * VISCOSITY / (12.0 * LENGTH_SPACING * LENGTH_SPACING))
                    first, second = walls[h, c, p, :, :128], walls[h, c, p, :, 128:]
                    reply[h * PARTS + n, c, p] = (second - v * first) + (dxx - u * dx)

    for j in (1, 3, 2, 0):
        chip = lax.rem(pair + j, CHUNKS)
        for copy in halo_copies(chip):
            copy.wait_recv()
        for core in range(2):
            finish(chip * 2 + core)
        for target in others(j):
            reply_copy(me, target).start()
    back[me] = reply[me]

    for j in (0, 1, 3, 2):
        for source in others(j):
            reply_copy(source, me).wait_recv()
    for c in range(3):
        for p in range(2):
            out[c, p] += back[:, c, p].reshape(128, 128).T

    for j in (1, 3, 2, 0):
        for target in others(j):
            out_copy(me, target).wait_send()
            reply_copy(me, target).wait_send()
        for copy in halo_copies(lax.rem(pair + j, CHUNKS)):
            copy.wait_send()


def solution(mesh):
    lines = mesh.shape["gx"] // 2

    def shards(velocity, previous):
        block = (3, 2, 128, 128)
        tiles = (RANKS, 3, 2, 8, 128)
        halo = (PARTS, 3, 2, 8, 128)
        f32 = jnp.float32
        table = operators()
        return pl.pallas_call(
            functools.partial(kernel, lines),
            out_shape=jax.ShapeDtypeStruct(block, f32),
            in_specs=[pl.BlockSpec(memory_space=pl.ANY)] * 3,
            out_specs=pl.BlockSpec(memory_space=pltpu.VMEM),
            scratch_shapes=[
                pltpu.VMEM(block, f32),
                pltpu.VMEM(block, f32),
                pltpu.VMEM(table.shape, jnp.bfloat16),
                pltpu.VMEM(tiles, f32),
                pltpu.VMEM(tiles, f32),
                pltpu.VMEM(halo, f32),
                pltpu.VMEM(halo, f32),
                pltpu.VMEM((PARTS, 96, 256), f32),
                pltpu.VMEM(tiles, f32),
                pltpu.VMEM(tiles, f32),
                pltpu.SemaphoreType.DMA((3,)),
                pltpu.SemaphoreType.DMA((RANKS,)),
                pltpu.SemaphoreType.DMA((RANKS,)),
                pltpu.SemaphoreType.DMA((2, CHUNKS)),
                pltpu.SemaphoreType.DMA((2, CHUNKS)),
                pltpu.SemaphoreType.DMA((RANKS,)),
                pltpu.SemaphoreType.DMA((RANKS,)),
            ],
            compiler_params=pltpu.CompilerParams(collective_id=0, has_side_effects=True),
        )(velocity, previous, jnp.asarray(table))

    spec = P(None, "gx", "gy", None)
    return jax.shard_map(shards, mesh=mesh, in_specs=(spec, spec), out_specs=spec, check_vma=False)
```

time: 223 us -> 49.1 us (0.22)
  other arithmetic: 105 us -> 0 us
  Pallas kernels: 0 us -> 47.2 us
  local copies, waits for them, and re-layouts: 41.2 us -> 1.77 us
  waiting for transfers between devices: 35 us -> 0 us
  starting transfers between devices: 30 us -> 0 us
  matrix products: 10.8 us -> 0 us
    reduce_sum x2 -> x0, other arithmetic: 65.2 us -> none  [the longest x1 32.8 us: chebyshev_rows(): jnp.sum(second_off, axis=1)[:, None]]
    pallas_call x0 -> x1, Pallas kernels: none -> 47.2 us  [shards(): pl.pallas_call(functools.partial(kernel, lines), out_shape=jax.ShapeDtype...]
    add x2 -> x0, other arithmetic: 37.1 us -> none  [the longest x1 35.1 us: chebyshev_rows(): first = first_off + jnp.where(on_diagonal, first_diag[:, None], 0.0)]
    all_to_all x2 -> x0, waiting for transfers between devices: 35 us -> none  [the longest x1 35 us: shards(): lax.all_to_all(joined, 'gy', split_axis=2, concat_axis=3, tiled=True)]
    unnamed x11 -> x1, local copies, waits for them, and re-layouts: 24.1 us -> 1.77 us
    all_to_all x2 -> x0, starting transfers between devices: 15.3 us -> none  [the longest x1 10.2 us: shards(): lax.all_to_all(velocity, 'gy', split_axis=3, concat_axis=2, tiled=True)]
    ppermute x2 -> x0, starting transfers between devices: 14.7 us -> none  [the longest x1 12.8 us: padded(): lax.ppermute(head, axis, [((i + 1) % count, i) for i in range(count)])]
    dot_general x1 -> x0, matrix products: 10.8 us -> none  [shards(): jnp.einsum('ky,cxyz->cxkz', operators, lax.all_to_all(velocity, 'gy', spl...]
  transfers between devices with their start and end apart: 4 -> 0, of which waited for: 1 -> 0; matrix products, arithmetic and copies ran while one was open for 56% -> 0% of each run, Pallas kernels for 0% -> 0%
where the time goes in v1:
time: 49.1 us; the launch traced here: 49 us
  Pallas kernels  47.2 us (96%)
  local copies, waits for them, and re-layouts  1.77 us (4%)
    pallas_call x1, Pallas kernels, shards(): pl.pallas_call(functools.partial(kernel, lines), out_shape=jax.ShapeDtype...  47.2 us
    unnamed x1, local copies, waits for them, and re-layouts  1.77 us

profile of v1, /device:TPU:1, one launch (start us, length us, event | category | flops | bytes accessed | tf_op | source)
XLA Modules:
  0.0 49.0 jit_solution(1558548672994001945)
XLA Ops:
  0.0 47.2 %shard_map.37 = f32[3,2,128,128]{3,2,1,0:T(8,128)} custom-call(f32[3,2,128,128]{3,2,1,0:T(8,128)} %vel_hbm.1, f32[3,2,128,128]{3,2,1,0:T(8,128)} %prev_hbm.1, bf16[2,4,8,256,256]{4,3,2,1,0:T(8,128)(2,1)} %constant.2.clone.op_hbm), custom_call_target="tpu_custom_call" | custom-call | tf_op jit(solution)/shard_map/pallas_call | solution.py:226
  47.2 1.8 %copy.5 = f32[3,2,128,128]{3,2,1,0:T(8,128)} copy(f32[3,2,128,128]{3,2,1,0:T(8,128)} %shard_map.37) | data formatting | bytes 786432

commit v2 on v1

v2 whole, which is shorter than its diff:
```python
import functools

import jax
import jax.numpy as jnp
import numpy as np
from jax import lax
from jax.experimental import pallas as pl
from jax.experimental.pallas import tpu as pltpu
from jax.sharding import PartitionSpec as P

NY = 1024
PARTS = 8
HALVES = 2
RANKS = PARTS * HALVES
CHUNKS = 4

LENGTH_SPACING = 8.0 * 3.141592653589793 / 4096.0
SPAN_SPACING = 3.0 * 3.141592653589793 / 3072.0
VISCOSITY = 1.0 / 2000.0
TIME_STEP = 0.003
GAMMA_NOW = 5.0 / 12.0
ZETA_PAST = -17.0 / 60.0
NOW = TIME_STEP * GAMMA_NOW
MESH = pl.DeviceIdType.MESH
GROUPS = ((0, 3),)
STAGES = (1, 3, 2, 0)


def chebyshev_rows(total):
    f32 = np.float32
    ids = np.arange(total)
    angle = ids.astype(f32) * (f32(np.pi) / f32(total - 1))
    on_diagonal = np.eye(total, dtype=bool)
    signs = (1.0 - 2.0 * ((ids[:, None] + ids[None, :]) % 2)).astype(f32)
    half = np.where((ids == 0) | (ids == total - 1), 0.5, 1.0).astype(f32)
    weight_ratio = signs * half[None, :] / half[:, None]
    plus = f32(0.5) * (angle[:, None] + angle[None, :])
    minus = f32(0.5) * (angle[:, None] - angle[None, :])
    spacing = f32(-2.0) * np.sin(plus) * np.sin(minus)
    safe = np.where(on_diagonal, f32(1.0), spacing)
    off = np.where(on_diagonal, f32(0.0), weight_ratio / safe).astype(np.float64)
    diag = -off.sum(axis=1)
    first = off + np.where(on_diagonal, diag[:, None], 0.0)
    off2 = np.where(on_diagonal, 0.0, 2.0 * off * (diag[:, None] - 1.0 / safe))
    second = off2 + np.where(on_diagonal, -off2.sum(axis=1)[:, None], 0.0)
    return first, second


@functools.lru_cache(maxsize=1)
def operators():
    first, second = chebyshev_rows(NY)
    first = (first * NOW).T.reshape(CHUNKS, 256, PARTS, 128)
    second = (second * (NOW * VISCOSITY)).T.reshape(CHUNKS, 256, PARTS, 128)
    both = np.concatenate([first, second], axis=3).transpose(0, 2, 1, 3)
    high = both.astype(np.float32).astype(jnp.bfloat16)
    low = (both - high.astype(np.float64)).astype(np.float32).astype(jnp.bfloat16)
    return np.stack([high, low])


def kernel(lines, vel_hbm, prev_hbm, op_hbm, out, vel, prev, op, send, recv, below, above, acc, reply, back,
           local_sem, send_sem, recv_sem, halo_send, halo_recv, reply_sem, back_sem):
    gx, gy = lax.axis_index("gx"), lax.axis_index("gy")
    line, half = gx // 2, gx % 2
    me = half * PARTS + gy
    pair = gy // 2
    nxt, prv = lax.rem(line + 1, lines), lax.rem(line + lines - 1, lines)

    def device(rank):
        return (line * 2 + rank // PARTS, lax.rem(rank, PARTS))

    load_vel = pltpu.make_async_copy(vel_hbm, vel, local_sem.at[0])
    load_prev = pltpu.make_async_copy(prev_hbm, prev, local_sem.at[1])
    load_op = pltpu.make_async_copy(op_hbm, op, local_sem.at[2])
    load_vel.start()
    load_prev.start()
    load_op.start()

    barrier = pltpu.get_barrier_semaphore()
    for k in range(1, RANKS):
        pl.semaphore_signal(barrier, inc=1, device_id=device(lax.rem(me + k, RANKS)), device_id_type=MESH)
    for other in (nxt, prv):
        pl.semaphore_signal(barrier, inc=1, device_id=(other * 2 + half, gy), device_id_type=MESH)

    load_vel.wait()
    for c in range(3):
        for p in range(2):
            send[:, c, p] = vel[c, p].T.reshape(RANKS, 8, 128)
    pl.semaphore_wait(barrier, RANKS + 1)

    def chip_at(shift):
        return lax.rem(pair + shift + CHUNKS, CHUNKS)

    def others(shift):
        found = []
        for h in range(HALVES):
            for core in range(2):
                if shift == 0 and h == 0 and core == 0:
                    continue
                hh = lax.rem(half + h, 2) if shift == 0 else h
                cc = lax.rem(gy + core, 2) if shift == 0 else core
                found.append(hh * PARTS + chip_at(shift) * 2 + cc)
        return found

    def out_copy(g, source, target):
        part = pl.ds(*GROUPS[g])
        return pltpu.make_async_remote_copy(
            src_ref=send.at[target, part], dst_ref=recv.at[source, part], send_sem=send_sem.at[g, target],
            recv_sem=recv_sem.at[g, source], device_id=device(target), device_id_type=MESH)

    def reply_copy(g, source, target):
        part = pl.ds(*GROUPS[g])
        return pltpu.make_async_remote_copy(
            src_ref=reply.at[target, part], dst_ref=back.at[source, part], send_sem=reply_sem.at[g, target],
            recv_sem=back_sem.at[g, source], device_id=device(target), device_id_type=MESH)

    def halo_copies(g, chip):
        part = pl.ds(*GROUPS[g])
        rows = pl.ds(chip * 2, 2)
        up = pltpu.make_async_remote_copy(
            src_ref=recv.at[pl.ds(PARTS + chip * 2, 2), part], dst_ref=below.at[rows, part],
            send_sem=halo_send.at[g, 0, chip], recv_sem=halo_recv.at[g, 0, chip],
            device_id=(nxt * 2 + half, gy), device_id_type=MESH)
        down = pltpu.make_async_remote_copy(
            src_ref=recv.at[rows, part], dst_ref=above.at[rows, part],
            send_sem=halo_send.at[g, 1, chip], recv_sem=halo_recv.at[g, 1, chip],
            device_id=(prv * 2 + half, gy), device_id_type=MESH)
        return up, down

    for g in range(len(GROUPS)):
        for j in STAGES:
            for target in others(-j):
                out_copy(g, me, target).start()
    recv[me] = send[me]

    load_prev.wait()
    for p in range(2):
        w = vel[2, p]
        for c in range(3):
            f = vel[c, p]
            up, down = pltpu.roll(f, 127, 1), pltpu.roll(f, 1, 1)
            up2, down2 = pltpu.roll(f, 126, 1), pltpu.roll(f, 2, 1)
            dz = (8.0 * (up - down) - (up2 - down2)) * (NOW / (12.0 * SPAN_SPACING))
            dzz = (16.0 * (up + down) - (up2 + down2) - 30.0 * f) * (
                NOW * VISCOSITY / (12.0 * SPAN_SPACING * SPAN_SPACING))
            out[c, p] = f + dzz - w * dz + (TIME_STEP * ZETA_PAST) * prev[c, p]
    load_op.wait()

    def products(g, chip):
        start, count = GROUPS[g]
        rows = 16 * count
        a = jnp.concatenate([
            jnp.concatenate([recv[h * PARTS + chip * 2 + core, start:start + count].reshape(rows, 128)
                             for core in range(2)], axis=1)
            for h in range(HALVES)], axis=0)
        high = a.astype(jnp.bfloat16)
        low = (a - high.astype(jnp.float32)).astype(jnp.bfloat16)
        stacked = jnp.concatenate([high, low], axis=0)

        def product(n):
            coarse = jnp.dot(stacked, op[0, chip, n], preferred_element_type=jnp.float32)
            fine = jnp.dot(high, op[1, chip, n], preferred_element_type=jnp.float32)
            return coarse[:2 * rows] + (coarse[2 * rows:] + fine)

        return product

    def rows_of(g):
        start, count = GROUPS[g]
        return pl.ds(32 * start, 32 * count)

    def finish(g, product, n):
        start, count = GROUPS[g]
        walls = (acc[n, rows_of(g)] + product(n)).reshape(HALVES, count, 2, 8, 256)
        columns = {}
        for c in {0, 1, *range(start, start + count)}:
            columns[c] = [below[n, c, 0], below[n, c, 1], recv[n, c, 0], recv[n, c, 1],
                          recv[PARTS + n, c, 0], recv[PARTS + n, c, 1], above[n, c, 0], above[n, c, 1]]
        for h in range(HALVES):
            for p in range(2):
                at = 2 + 2 * h + p
                u, v = columns[0][at], columns[1][at]
                for i in range(count):
                    f = columns[start + i]
                    dx = (8.0 * (f[at + 1] - f[at - 1]) - (f[at + 2] - f[at - 2])) * (
                        NOW / (12.0 * LENGTH_SPACING))
                    dxx = (16.0 * (f[at + 1] + f[at - 1]) - (f[at + 2] + f[at - 2]) - 30.0 * f[at]) * (
                        NOW * VISCOSITY / (12.0 * LENGTH_SPACING * LENGTH_SPACING))
                    first, second = walls[h, i, p, :, :128], walls[h, i, p, :, 128:]
                    reply[h * PARTS + n, start + i, p] = (second - v * first) + (dxx - u * dx)

    for g in range(len(GROUPS)):
        for step, j in enumerate(STAGES):
            chip = chip_at(j)
            for source in others(j):
                out_copy(g, source, me).wait_recv()
            for copy in halo_copies(g, chip):
                copy.start()
            product = products(g, chip)
            if step < CHUNKS - 1:
                @pl.loop(0, PARTS)
                def _(n, product=product, step=step, g=g):
                    if step == 0:
                        acc[n, rows_of(g)] = product(n)
                    else:
                        acc[n, rows_of(g)] += product(n)
        for j in STAGES:
            chip = chip_at(j)
            for copy in halo_copies(g, chip):
                copy.wait_recv()
            for core in range(2):
                finish(g, product, chip * 2 + core)
            for target in others(j):
                reply_copy(g, me, target).start()
    back[me] = reply[me]

    for g, (start, count) in enumerate(GROUPS):
        for j in STAGES:
            for source in others(j):
                reply_copy(g, source, me).wait_recv()
        for c in range(start, start + count):
            for p in range(2):
                out[c, p] += back[:, c, p].reshape(128, 128).T

    for g in range(len(GROUPS)):
        for j in STAGES:
            for target in others(j):
                out_copy(g, me, target).wait_send()
                reply_copy(g, me, target).wait_send()
            for copy in halo_copies(g, chip_at(j)):
                copy.wait_send()


def solution(mesh):
    lines = mesh.shape["gx"] // 2

    def shards(velocity, previous):
        block = (3, 2, 128, 128)
        tiles = (RANKS, 3, 2, 8, 128)
        halo = (PARTS, 3, 2, 8, 128)
        f32 = jnp.float32
        table = operators()
        groups = len(GROUPS)
        return pl.pallas_call(
            functools.partial(kernel, lines),
            out_shape=jax.ShapeDtypeStruct(block, f32),
            in_specs=[pl.BlockSpec(memory_space=pl.ANY)] * 3,
            out_specs=pl.BlockSpec(memory_space=pltpu.VMEM),
            scratch_shapes=[
                pltpu.VMEM(block, f32),
                pltpu.VMEM(block, f32),
                pltpu.VMEM(table.shape, jnp.bfloat16),
                pltpu.VMEM(tiles, f32),
                pltpu.VMEM(tiles, f32),
                pltpu.VMEM(halo, f32),
                pltpu.VMEM(halo, f32),
                pltpu.VMEM((PARTS, 96, 256), f32),
                pltpu.VMEM(tiles, f32),
                pltpu.VMEM(tiles, f32),
                pltpu.SemaphoreType.DMA((3,)),
                pltpu.SemaphoreType.DMA((groups, RANKS)),
                pltpu.SemaphoreType.DMA((groups, RANKS)),
                pltpu.SemaphoreType.DMA((groups, 2, CHUNKS)),
                pltpu.SemaphoreType.DMA((groups, 2, CHUNKS)),
                pltpu.SemaphoreType.DMA((groups, RANKS)),
                pltpu.SemaphoreType.DMA((groups, RANKS)),
            ],
            compiler_params=pltpu.CompilerParams(collective_id=0, has_side_effects=True),
        )(velocity, previous, jnp.asarray(table))

    spec = P(None, "gx", "gy", None)
    return jax.shard_map(shards, mesh=mesh, in_specs=(spec, spec), out_specs=spec, check_vma=False)
```

time: 49.1 us -> 43.2 us (0.88)
  Pallas kernels: 47.2 us -> 41.3 us
    pallas_call x1, Pallas kernels: 47.2 us -> 41.3 us  [shards(): pl.pallas_call(functools.partial(kernel, lines), out_shape=jax.ShapeDtype...]
where the time goes in v2:
time: 43.2 us; the launch traced here: 43.1 us
  Pallas kernels  41.3 us (96%)
  local copies, waits for them, and re-layouts  1.77 us (4%)
    pallas_call x1, Pallas kernels, shards(): pl.pallas_call(functools.partial(kernel, lines), out_shape=jax.ShapeDtype...  41.3 us
    unnamed x1, local copies, waits for them, and re-layouts  1.77 us

profile of v2, /device:TPU:1, one launch (start us, length us, event | category | flops | bytes accessed | tf_op | source)
XLA Modules:
  0.0 43.1 jit_solution(17811361011108422676)
XLA Ops:
  0.0 41.3 %shard_map.37 = f32[3,2,128,128]{3,2,1,0:T(8,128)} custom-call(f32[3,2,128,128]{3,2,1,0:T(8,128)} %vel_hbm.1, f32[3,2,128,128]{3,2,1,0:T(8,128)} %prev_hbm.1, bf16[2,4,8,256,256]{4,3,2,1,0:T(8,128)(2,1)} %constant.2.clone.op_hbm), custom_call_target="tpu_custom_call" | custom-call | tf_op jit(solution)/shard_map/pallas_call | solution.py:242
  41.3 1.8 %copy.5 = f32[3,2,128,128]{3,2,1,0:T(8,128)} copy(f32[3,2,128,128]{3,2,1,0:T(8,128)} %shard_map.37) | data formatting | bytes 786432

commit v3 on v1

v3 whole, which is shorter than its diff:
```python
import functools

import jax
import jax.numpy as jnp
import numpy as np
from jax import lax
from jax.experimental import pallas as pl
from jax.experimental.pallas import tpu as pltpu
from jax.sharding import PartitionSpec as P

NY = 1024
PARTS = 8
HALVES = 2
RANKS = PARTS * HALVES
DEPTH = 8
CHUNKS = 4

LENGTH_SPACING = 8.0 * 3.141592653589793 / 4096.0
SPAN_SPACING = 3.0 * 3.141592653589793 / 3072.0
VISCOSITY = 1.0 / 2000.0
TIME_STEP = 0.003
GAMMA_NOW = 5.0 / 12.0
ZETA_PAST = -17.0 / 60.0
NOW = TIME_STEP * GAMMA_NOW
MESH = pl.DeviceIdType.MESH
STAGES = (1, 3, 2, 0)


def chebyshev_rows(total):
    f32 = np.float32
    ids = np.arange(total)
    angle = ids.astype(f32) * (f32(np.pi) / f32(total - 1))
    on_diagonal = np.eye(total, dtype=bool)
    signs = (1.0 - 2.0 * ((ids[:, None] + ids[None, :]) % 2)).astype(f32)
    half = np.where((ids == 0) | (ids == total - 1), 0.5, 1.0).astype(f32)
    weight_ratio = signs * half[None, :] / half[:, None]
    plus = f32(0.5) * (angle[:, None] + angle[None, :])
    minus = f32(0.5) * (angle[:, None] - angle[None, :])
    spacing = f32(-2.0) * np.sin(plus) * np.sin(minus)
    safe = np.where(on_diagonal, f32(1.0), spacing)
    off = np.where(on_diagonal, f32(0.0), weight_ratio / safe).astype(np.float64)
    diag = -off.sum(axis=1)
    first = off + np.where(on_diagonal, diag[:, None], 0.0)
    off2 = np.where(on_diagonal, 0.0, 2.0 * off * (diag[:, None] - 1.0 / safe))
    second = off2 + np.where(on_diagonal, -off2.sum(axis=1)[:, None], 0.0)
    return first, second


@functools.lru_cache(maxsize=1)
def operators():
    first, second = chebyshev_rows(NY)
    first = (first * NOW).T.reshape(CHUNKS, 256, PARTS, 128)
    second = (second * (NOW * VISCOSITY)).T.reshape(CHUNKS, 256, PARTS, 128)
    both = np.concatenate([first, second], axis=3).transpose(0, 2, 1, 3)
    high = both.astype(np.float32).astype(jnp.bfloat16)
    low = (both - high.astype(np.float64)).astype(np.float32).astype(jnp.bfloat16)
    return np.stack([high, low])


def kernel(lines, vel_hbm, prev_hbm, op_hbm, out, vel, prev, op, send, slab, acc, reply, back,
           local_sem, send_sem, recv_sem, halo_send, halo_recv, reply_sem, back_sem, direct_sem, ready_sem):
    gx, gy = lax.axis_index("gx"), lax.axis_index("gy")
    line, half = gx // 2, gx % 2
    me = half * PARTS + gy
    pair = gy // 2
    nxt, prv = lax.rem(line + 1, lines), lax.rem(line + lines - 1, lines)
    period = min(DEPTH, lines)
    wrapped = 1 - (lax.rem(line, period) + period - 1) // period
    last = (lax.rem(line, period) + 1) // period

    def device(rank):
        return (line * 2 + rank // PARTS, lax.rem(rank, PARTS))

    load_vel = pltpu.make_async_copy(vel_hbm, vel, local_sem.at[0])
    load_prev = pltpu.make_async_copy(prev_hbm, prev, local_sem.at[1])
    load_op = pltpu.make_async_copy(op_hbm, op, local_sem.at[2])
    load_vel.start()
    load_prev.start()
    load_op.start()

    barrier = pltpu.get_barrier_semaphore()
    for k in range(1, RANKS):
        pl.semaphore_signal(barrier, inc=1, device_id=device(lax.rem(me + k, RANKS)), device_id_type=MESH)
    pl.semaphore_signal(barrier, inc=1, device_id=(prv * 2 + half, gy), device_id_type=MESH)

    @pl.when(last == 0)
    def _():
        pl.semaphore_signal(barrier, inc=1, device_id=(nxt * 2 + half, gy), device_id_type=MESH)

    @pl.when(wrapped == 1)
    def _():
        for b in range(PARTS):
            pl.semaphore_signal(barrier, inc=1, device_id=(prv * 2 + 1, b), device_id_type=MESH)

    load_vel.wait()
    for c in range(3):
        for p in range(2):
            send[:, c, p] = vel[c, p].T.reshape(RANKS, 8, 128)
    pl.semaphore_wait(barrier, RANKS + 1 - wrapped + RANKS * last * half)

    @pl.when(last == 1)
    def _():
        pl.semaphore_signal(ready_sem, inc=1, device_id=(nxt * 2 + half, gy), device_id_type=MESH)

    def chip_at(shift):
        return lax.rem(pair + shift + CHUNKS, CHUNKS)

    def others(shift):
        found = []
        for h in range(HALVES):
            for core in range(2):
                if shift == 0 and h == 0 and core == 0:
                    continue
                hh = lax.rem(half + h, 2) if shift == 0 else h
                cc = lax.rem(gy + core, 2) if shift == 0 else core
                found.append(hh * PARTS + chip_at(shift) * 2 + cc)
        return found

    def out_copy(source, target):
        return pltpu.make_async_remote_copy(
            src_ref=send.at[target], dst_ref=slab.at[1 + source // PARTS, lax.rem(source, PARTS)],
            send_sem=send_sem.at[target], recv_sem=recv_sem.at[source], device_id=device(target),
            device_id_type=MESH)

    def reply_copy(source, target):
        return pltpu.make_async_remote_copy(
            src_ref=reply.at[target], dst_ref=back.at[source], send_sem=reply_sem.at[target],
            recv_sem=back_sem.at[source], device_id=device(target), device_id_type=MESH)

    def up_copy(chip):
        rows = pl.ds(chip * 2, 2)
        return pltpu.make_async_remote_copy(
            src_ref=slab.at[2, rows], dst_ref=slab.at[0, rows], send_sem=halo_send.at[0, chip],
            recv_sem=halo_recv.at[0, chip], device_id=(nxt * 2 + half, gy), device_id_type=MESH)

    def down_copy(chip):
        rows = pl.ds(chip * 2, 2)
        return pltpu.make_async_remote_copy(
            src_ref=slab.at[1, rows], dst_ref=slab.at[3, rows], send_sem=halo_send.at[1, chip],
            recv_sem=halo_recv.at[1, chip], device_id=(prv * 2 + half, gy), device_id_type=MESH)

    def direct_copy(target):
        return pltpu.make_async_remote_copy(
            src_ref=send.at[target], dst_ref=slab.at[0, gy], send_sem=direct_sem.at[target],
            recv_sem=halo_recv.at[0, pair], device_id=(nxt * 2 + target // PARTS, lax.rem(target, PARTS)),
            device_id_type=MESH)

    def everyone(shift):
        return [h * PARTS + chip_at(shift) * 2 + core for h in range(HALVES) for core in range(2)]

    def halo_wait(h, chip):
        rows = pl.ds(chip * 2, 2)
        pltpu.make_async_remote_copy(
            src_ref=slab.at[1, rows], dst_ref=slab.at[h * 3, rows], send_sem=halo_send.at[h, chip],
            recv_sem=halo_recv.at[h, chip], device_id=(prv * 2 + half, gy), device_id_type=MESH).wait_recv()

    @pl.when(last * half == 1)
    def _():
        for j in STAGES:
            for target in everyone(-j):
                direct_copy(target).start()

    for j in STAGES:
        for target in others(-j):
            out_copy(me, target).start()
    slab[1 + half, gy] = send[me]

    load_prev.wait()
    for p in range(2):
        w = vel[2, p]
        for c in range(3):
            f = vel[c, p]
            up, down = pltpu.roll(f, 127, 1), pltpu.roll(f, 1, 1)
            up2, down2 = pltpu.roll(f, 126, 1), pltpu.roll(f, 2, 1)
            dz = (8.0 * (up - down) - (up2 - down2)) * (NOW / (12.0 * SPAN_SPACING))
            dzz = (16.0 * (up + down) - (up2 + down2) - 30.0 * f) * (
                NOW * VISCOSITY / (12.0 * SPAN_SPACING * SPAN_SPACING))
            out[c, p] = f + dzz - w * dz + (TIME_STEP * ZETA_PAST) * prev[c, p]
    load_op.wait()

    for step, j in enumerate(STAGES):
        chip = chip_at(j)
        for source in others(j):
            out_copy(source, me).wait_recv()

        @pl.when(last == 0)
        def _(chip=chip):
            up_copy(chip).start()

        @pl.when(wrapped == 0)
        def _(chip=chip):
            down_copy(chip).start()

        a = jnp.concatenate([
            jnp.concatenate([slab[1 + h, chip * 2 + core].reshape(48, 128) for core in range(2)], axis=1)
            for h in range(HALVES)], axis=0)
        high = a.astype(jnp.bfloat16)
        low = (a - high.astype(jnp.float32)).astype(jnp.bfloat16)
        stacked = jnp.concatenate([high, low], axis=0)

        @pl.loop(0, PARTS, unroll=8)
        def _(n, step=step, chip=chip, stacked=stacked, high=high):
            coarse = jnp.dot(stacked, op[0, chip, n], preferred_element_type=jnp.float32)
            fine = jnp.dot(high, op[1, chip, n], preferred_element_type=jnp.float32)
            product = (coarse[:96] + (coarse[96:] + fine)).reshape(HALVES, 48, 256)
            if step == 0:
                acc[:, n] = product
            else:
                acc[:, n] += product

    def finish(h, n):
        walls = acc[h, n].reshape(3, 2, 8, 256)
        planes = [[slab[h + q // 2, n, c, q % 2] for q in range(6)] for c in range(3)]
        for p in range(2):
            at = 2 + p
            u, v = planes[0][at], planes[1][at]
            for c in range(3):
                f = planes[c]
                dx = (8.0 * (f[at + 1] - f[at - 1]) - (f[at + 2] - f[at - 2])) * (NOW / (12.0 * LENGTH_SPACING))
                dxx = (16.0 * (f[at + 1] + f[at - 1]) - (f[at + 2] + f[at - 2]) - 30.0 * f[at]) * (
                    NOW * VISCOSITY / (12.0 * LENGTH_SPACING * LENGTH_SPACING))
                first, second = walls[c, p, :, :128], walls[c, p, :, 128:]
                reply[h * PARTS + n, c, p] = (second - v * first) + (dxx - u * dx)

    @pl.when(wrapped == 1)
    def _():
        pl.semaphore_wait(ready_sem, 1)
        for j in STAGES:
            down_copy(chip_at(j)).start()

    for j in STAGES:
        chip = chip_at(j)
        for h in range(HALVES):
            halo_wait(h, chip)
        for core in range(2):
            for h in range(HALVES):
                finish(h, chip * 2 + core)
        for target in others(j):
            reply_copy(me, target).start()
    back[me] = reply[me]

    for j in STAGES:
        for source in others(j):
            reply_copy(source, me).wait_recv()
    for c in range(3):
        for p in range(2):
            out[c, p] += back[:, c, p].reshape(128, 128).T

    for j in STAGES:
        for target in others(j):
            out_copy(me, target).wait_send()
            reply_copy(me, target).wait_send()
        down_copy(chip_at(j)).wait_send()

    @pl.when(last == 0)
    def _():
        for j in STAGES:
            up_copy(chip_at(j)).wait_send()

    @pl.when(last * half == 1)
    def _():
        for target in range(RANKS):
            direct_copy(target).wait_send()


def solution(mesh):
    lines = mesh.shape["gx"] // 2

    def shards(velocity, previous):
        block = (3, 2, 128, 128)
        tiles = (RANKS, 3, 2, 8, 128)
        f32 = jnp.float32
        table = operators()
        return pl.pallas_call(
            functools.partial(kernel, lines),
            out_shape=jax.ShapeDtypeStruct(block, f32),
            in_specs=[pl.BlockSpec(memory_space=pl.ANY)] * 3,
            out_specs=pl.BlockSpec(memory_space=pltpu.VMEM),
            scratch_shapes=[
                pltpu.VMEM(block, f32),
                pltpu.VMEM(block, f32),
                pltpu.VMEM(table.shape, jnp.bfloat16),
                pltpu.VMEM(tiles, f32),
                pltpu.VMEM((4, PARTS, 3, 2, 8, 128), f32),
                pltpu.VMEM((HALVES, PARTS, 48, 256), f32),
                pltpu.VMEM(tiles, f32),
                pltpu.VMEM(tiles, f32),
                pltpu.SemaphoreType.DMA((3,)),
                pltpu.SemaphoreType.DMA((RANKS,)),
                pltpu.SemaphoreType.DMA((RANKS,)),
                pltpu.SemaphoreType.DMA((2, CHUNKS)),
                pltpu.SemaphoreType.DMA((2, CHUNKS)),
                pltpu.SemaphoreType.DMA((RANKS,)),
                pltpu.SemaphoreType.DMA((RANKS,)),
                pltpu.SemaphoreType.DMA((RANKS,)),
                pltpu.SemaphoreType.REGULAR,
            ],
            compiler_params=pltpu.CompilerParams(collective_id=0, has_side_effects=True),
        )(velocity, previous, jnp.asarray(table))

    spec = P(None, "gx", "gy", None)
    return jax.shard_map(shards, mesh=mesh, in_specs=(spec, spec), out_specs=spec, check_vma=False)
```

time: 49.1 us -> 40.1 us (0.82)
  the two profiles are of different devices: /device:TPU:1 before, /device:TPU:451 now
where the time goes in v3:
time: 40.1 us; the launch traced here: 40 us
  Pallas kernels  38.2 us (95%)
  local copies, waits for them, and re-layouts  1.77 us (4%)
    pallas_call x1, Pallas kernels, shards(): pl.pallas_call(functools.partial(kernel, lines), out_shape=jax.ShapeDtype...  38.2 us
    unnamed x1, local copies, waits for them, and re-layouts  1.77 us

profile of v3, /device:TPU:451, one launch (start us, length us, event | category | flops | bytes accessed | tf_op | source)
XLA Modules:
  0.0 40.0 jit_solution(14904392312333414246)
XLA Ops:
  0.0 38.2 %shard_map.37 = f32[3,2,128,128]{3,2,1,0:T(8,128)} custom-call(f32[3,2,128,128]{3,2,1,0:T(8,128)} %vel_hbm.1, f32[3,2,128,128]{3,2,1,0:T(8,128)} %prev_hbm.1, bf16[2,4,8,256,256]{4,3,2,1,0:T(8,128)(2,1)} %constant.2.clone.op_hbm), custom_call_target="tpu_custom_call" | custom-call | tf_op jit(solution)/shard_map/pallas_call | solution.py:274
  38.2 1.8 %copy.5 = f32[3,2,128,128]{3,2,1,0:T(8,128)} copy(f32[3,2,128,128]{3,2,1,0:T(8,128)} %shard_map.37) | data formatting | bytes 786432

commit v4 on v3

--- a/solution.py
+++ b/solution.py
@@ -295,8 +295,8 @@
                 pltpu.SemaphoreType.DMA((RANKS,)),
                 pltpu.SemaphoreType.REGULAR,
             ],
-            compiler_params=pltpu.CompilerParams(collective_id=0, has_side_effects=True),
-        )(velocity, previous, jnp.asarray(table))
+            compiler_params=pltpu.CompilerParams(collective_id=0, has_side_effects=True, vmem_limit_bytes=24 << 20),
+        )(*[pltpu.with_memory_space_constraint(x, pltpu.HBM) for x in (velocity, previous, jnp.asarray(table))])
 
     spec = P(None, "gx", "gy", None)
     return jax.shard_map(shards, mesh=mesh, in_specs=(spec, spec), out_specs=spec, check_vma=False)

time: 40.1 us -> 38.3 us (0.955)
  local copies, waits for them, and re-layouts: 1.77 us -> 0.75 us
  Pallas kernels: 38.2 us -> 37.4 us
    unnamed x1, local copies, waits for them, and re-layouts: 1.77 us -> 0.75 us
    pallas_call x1, Pallas kernels: 38.2 us -> 37.4 us  [shards(): pl.pallas_call(functools.partial(kernel, lines), out_shape=jax.ShapeDtype...]
where the time goes in v4:
time: 38.3 us; the launch traced here: 38.2 us
  Pallas kernels  37.4 us (98%)
  local copies, waits for them, and re-layouts  0.75 us (2%)
    pallas_call x1, Pallas kernels, shards(): pl.pallas_call(functools.partial(kernel, lines), out_shape=jax.ShapeDtype...  37.4 us

profile of v4, /device:TPU:451, one launch (start us, length us, event | category | flops | bytes accessed | tf_op | source)
XLA Modules:
  0.0 38.2 jit_solution(9801542660745053874)
XLA Ops:
  0.0 37.4 %shard_map.37 = f32[3,2,128,128]{3,2,1,0:T(8,128)S(1)} custom-call(f32[3,2,128,128]{3,2,1,0:T(8,128)} %vel_hbm.1, f32[3,2,128,128]{3,2,1,0:T(8,128)} %prev_hbm.1, bf16[2,4,8,256,256]{4,3,2,1,0:T(8,128)(2,1)} %constant.2.clone.op_hbm), custom_call_target="tpu_custom_call" | custom-call | tf_op jit(solution)/shard_map/pallas_call | solution.py:274
  37.5 0.7 %copy.5 = f32[3,2,128,128]{3,2,1,0:T(8,128)} copy(f32[3,2,128,128]{3,2,1,0:T(8,128)S(1)} %shard_map.37) | data formatting | bytes 786432

commit v5 on v4

--- a/solution.py
+++ b/solution.py
@@ -23,7 +23,7 @@
 ZETA_PAST = -17.0 / 60.0
 NOW = TIME_STEP * GAMMA_NOW
 MESH = pl.DeviceIdType.MESH
-STAGES = (1, 3, 2, 0)
+STAGES = (0, 1, 3, 2)
 
 
 def chebyshev_rows(total):

time: 38.3 us -> 36.5 us (0.953)
  the two profiles are of different devices: /device:TPU:451 before, /device:TPU:453 now
where the time goes in v5:
time: 36.5 us; the launch traced here: 36.3 us
  Pallas kernels  35.6 us (98%)
  local copies, waits for them, and re-layouts  0.75 us (2%)
    pallas_call x1, Pallas kernels, shards(): pl.pallas_call(functools.partial(kernel, lines), out_shape=jax.ShapeDtype...  35.6 us
    unnamed x1, local copies, waits for them, and re-layouts  0.75 us

profile of v5, /device:TPU:453, one launch (start us, length us, event | category | flops | bytes accessed | tf_op | source)
XLA Modules:
  0.0 36.3 jit_solution(5746902585710853857)
XLA Ops:
  0.0 35.6 %shard_map.37 = f32[3,2,128,128]{3,2,1,0:T(8,128)S(1)} custom-call(f32[3,2,128,128]{3,2,1,0:T(8,128)} %vel_hbm.1, f32[3,2,128,128]{3,2,1,0:T(8,128)} %prev_hbm.1, bf16[2,4,8,256,256]{4,3,2,1,0:T(8,128)(2,1)} %constant.2.clone.op_hbm), custom_call_target="tpu_custom_call" | custom-call | tf_op jit(solution)/shard_map/pallas_call | solution.py:274
  35.6 0.7 %copy.5 = f32[3,2,128,128]{3,2,1,0:T(8,128)} copy(f32[3,2,128,128]{3,2,1,0:T(8,128)S(1)} %shard_map.37) | data formatting | bytes 786432

commit v6 on v5

--- a/solution.py
+++ b/solution.py
@@ -79,14 +79,14 @@
     load_op.start()
 
     barrier = pltpu.get_barrier_semaphore()
+    pl.semaphore_signal(barrier, inc=1, device_id=(prv * 2 + half, gy), device_id_type=MESH)
+
+    @pl.when(last == 0)
+    def _():
+        pl.semaphore_signal(barrier, inc=1, device_id=(nxt * 2 + half, gy), device_id_type=MESH)
+
     for k in range(1, RANKS):
         pl.semaphore_signal(barrier, inc=1, device_id=device(lax.rem(me + k, RANKS)), device_id_type=MESH)
-    pl.semaphore_signal(barrier, inc=1, device_id=(prv * 2 + half, gy), device_id_type=MESH)
-
-    @pl.when(last == 0)
-    def _():
-        pl.semaphore_signal(barrier, inc=1, device_id=(nxt * 2 + half, gy), device_id_type=MESH)
-
     @pl.when(wrapped == 1)
     def _():
         for b in range(PARTS):
@@ -198,8 +198,7 @@
         low = (a - high.astype(jnp.float32)).astype(jnp.bfloat16)
         stacked = jnp.concatenate([high, low], axis=0)
 
-        @pl.loop(0, PARTS, unroll=8)
-        def _(n, step=step, chip=chip, stacked=stacked, high=high):
+        def accumulate(n, step=step, chip=chip, stacked=stacked, high=high):
             coarse = jnp.dot(stacked, op[0, chip, n], preferred_element_type=jnp.float32)
             fine = jnp.dot(high, op[1, chip, n], preferred_element_type=jnp.float32)
             product = (coarse[:96] + (coarse[96:] + fine)).reshape(HALVES, 48, 256)
@@ -207,6 +206,9 @@
                 acc[:, n] = product
             else:
                 acc[:, n] += product
+
+        if step < CHUNKS - 1:
+            pl.loop(0, PARTS, unroll=8)(accumulate)
 
     def finish(h, n):
         walls = acc[h, n].reshape(3, 2, 8, 256)
@@ -232,6 +234,8 @@
         chip = chip_at(j)
         for h in range(HALVES):
             halo_wait(h, chip)
+        for core in range(2):
+            accumulate(chip * 2 + core)
         for core in range(2):
             for h in range(HALVES):
                 finish(h, chip * 2 + core)

time: 36.5 us -> 37.5 us (1.027)
  Pallas kernels: 35.6 us -> 36.6 us
    pallas_call x1, Pallas kernels: 35.6 us -> 36.6 us  [shards(): pl.pallas_call(functools.partial(kernel, lines), out_shape=jax.ShapeDtype...]
where the time goes in v6:
time: 37.5 us; the launch traced here: 37.3 us
  Pallas kernels  36.6 us (98%)
  local copies, waits for them, and re-layouts  0.75 us (2%)
    pallas_call x1, Pallas kernels, shards(): pl.pallas_call(functools.partial(kernel, lines), out_shape=jax.ShapeDtype...  36.6 us

profile of v6, /device:TPU:453, one launch (start us, length us, event | category | flops | bytes accessed | tf_op | source)
XLA Modules:
  0.0 37.3 jit_solution(89313132634133472)
XLA Ops:
  0.0 36.6 %shard_map.37 = f32[3,2,128,128]{3,2,1,0:T(8,128)S(1)} custom-call(f32[3,2,128,128]{3,2,1,0:T(8,128)} %vel_hbm.1, f32[3,2,128,128]{3,2,1,0:T(8,128)} %prev_hbm.1, bf16[2,4,8,256,256]{4,3,2,1,0:T(8,128)(2,1)} %constant.2.clone.op_hbm), custom_call_target="tpu_custom_call" | custom-call | tf_op jit(solution)/shard_map/pallas_call | solution.py:278
  36.6 0.7 %copy.5 = f32[3,2,128,128]{3,2,1,0:T(8,128)} copy(f32[3,2,128,128]{3,2,1,0:T(8,128)S(1)} %shard_map.37) | data formatting | bytes 786432
